TPU v7x, 512 devices: a whole 4x4x16 slice. The times are simulated.
512 devices in a mesh: grp: 8 (over x, core), own: 64 (over z, y).
Axes of the slice: x: 4, y: 4, z: 16, core: 2. Of those that a mesh axis runs over, the one named last changes fastest.
Arguments:
- left: bfloat16 [32768, 128, 64], P(('grp', 'own')), may hold values from -0.75 to 0.75
- right: bfloat16 [32768, 128, 64], P(('grp', 'own')), may hold values from -0.75 to 0.75
- values: bfloat16 [32768, 128], P(('grp', 'own')), may hold values from -6 to 6
- core: bfloat16 [10240, 64, 64], P(('grp', 'own')), may hold values from -6 to 6
- tile_slice: int32 [32768], P(('grp', 'own')), may hold values from 0 to 10239, as said below
- tile_fill: int32 [32768], P(('grp', 'own')), may hold values from 64 to 128
Outputs:
- new_core: bfloat16 [10240, 64, 64], P(('grp', 'own'))
- new_left: bfloat16 [32768, 128, 64], P(('grp', 'own'))
Inputs may be any that keep to these rules, and one draw needn't show every extreme that they name: `tile_slice`: call j // 20 the block of slice j and its remainder mod 64 its class. Among the tiles of one device at most 2 have slices of one class; in every group of 64 consecutive devices some class gets exactly 2 tiles from every device of the group.
All inputs are finite; a program needn't handle non-finite values.
Results may differ from a plain program's by a relative error of at most 0.0052.
Values may be sent and summed in bfloat16 or wider, within the bound.
No kernel may reach another device: no remote copies, remote signals or barrier semaphores. Data moves between devices by JAX's collectives and lax.ppermute only.
A program may use at most 64 MiB of HBM per device.

v0:
```python
import jax
import jax.numpy as jnp
from jax import lax
from jax.sharding import PartitionSpec as P


def tile_terms(left_tiles, right_tiles, value_tiles, fill_counts, slice_tables):
    tile_rows = left_tiles.shape[1]
    projected = jnp.einsum(
        "sea,sab->seb", left_tiles, slice_tables, preferred_element_type=jnp.float32
    )
    predicted = jnp.sum(projected * right_tiles.astype(jnp.float32), axis=-1)
    live_rows = jnp.arange(tile_rows)[None, :] < fill_counts[:, None]
    residual = jnp.where(live_rows, predicted - value_tiles.astype(jnp.float32), 0.0)
    weighted = (residual[:, :, None] * left_tiles.astype(jnp.float32)).astype(jnp.bfloat16)
    return jnp.einsum("sea,seb->sab", weighted, right_tiles, preferred_element_type=jnp.float32)


def body(left, right, values, core, tile_slice, tile_fill):
    owners = lax.axis_size("own")
    groups = lax.axis_size("grp")
    tile_count, tile_rows, rank_width = left.shape
    per_device = core.shape[0]
    local_count = groups * per_device
    slot_cap = 2 * tile_count // owners
    slot_total = owners * slot_cap
    dev_block = tile_slice // per_device
    target_owner = dev_block % owners
    local_slice = dev_block // owners * per_device + tile_slice % per_device
    positions = jnp.arange(tile_count)
    same_owner = target_owner[:, None] == target_owner[None, :]
    earlier = positions[None, :] < positions[:, None]
    rank_among = jnp.sum((same_owner & earlier).astype(jnp.int32), axis=1)
    slot_of_tile = target_owner * slot_cap + rank_among
    slot_match = slot_of_tile[None, :] == jnp.arange(slot_total)[:, None]
    slot_live = jnp.any(slot_match, axis=1)
    tile_of_slot = jnp.sum(jnp.where(slot_match, positions[None, :], 0), axis=1)
    send_slice = jnp.where(slot_live, local_slice[tile_of_slot], 0)
    old_tables = lax.all_gather(core, "grp", axis=0, tiled=True)
    send_left = left[tile_of_slot]
    send_right = right[tile_of_slot]
    send_values = values[tile_of_slot]
    send_fill = jnp.where(slot_live, tile_fill[tile_of_slot], 0)
    got_left, got_right, got_values, got_slice, got_fill = (
        lax.all_to_all(send_left, "own", split_axis=0, concat_axis=0, tiled=True),
        lax.all_to_all(send_right, "own", split_axis=0, concat_axis=0, tiled=True),
        lax.all_to_all(send_values, "own", split_axis=0, concat_axis=0, tiled=True),
        lax.all_to_all(send_slice, "own", split_axis=0, concat_axis=0, tiled=True),
        lax.all_to_all(send_fill, "own", split_axis=0, concat_axis=0, tiled=True),
    )
    tile_grad = tile_terms(got_left, got_right, got_values, got_fill, old_tables[got_slice])
    selector = (got_slice[:, None] == jnp.arange(local_count)[None, :]).astype(jnp.float32)
    grad_part = jnp.dot(
        selector.T,
        tile_grad.reshape(slot_total, rank_width * rank_width),
        precision=lax.Precision.HIGHEST,
        preferred_element_type=jnp.float32,
    ).reshape(local_count, rank_width, rank_width)
    grad_whole = lax.psum(grad_part, "grp")
    new_tables = (old_tables.astype(jnp.float32) - grad_whole).astype(jnp.bfloat16)
    new_mine = lax.dynamic_slice_in_dim(
        new_tables, lax.axis_index("grp") * per_device, per_device, 0
    )
    refreshed = jnp.einsum(
        "sea,sab->seb", got_left, new_tables[got_slice], preferred_element_type=jnp.float32
    ).astype(jnp.bfloat16)
    returned = lax.all_to_all(refreshed, "own", split_axis=0, concat_axis=0, tiled=True)
    new_left = returned[slot_of_tile]
    return (new_mine, new_left)


def solution(mesh):
    return jax.shard_map(
        body,
        mesh=mesh,
        in_specs=(
            P(("grp", "own"), None, None),
            P(("grp", "own"), None, None),
            P(("grp", "own"), None),
            P(("grp", "own"), None, None),
            P(("grp", "own")),
            P(("grp", "own")),
        ),
        out_specs=(P(("grp", "own"), None, None), P(("grp", "own"), None, None)),
        check_vma=False,
    )
```

profile of v0, /device:TPU:7, one launch (start us, length us, event | category | flops | bytes accessed | tf_op | source)
XLA Modules:
  0.0 528.3 jit_solution(8652673713095691326)
XLA Ops:
  9.6 1.6 gather_fusion.1
  12.0 18.5 %all-to-all-start.1 = ((s32[64,2,1]{1,2,0:T(1,128)}), s32[64,2,1]{1,2,0:T(1,128)S(1)}, u32[]{:S(2)}, u32[]{:S(2)}) async-start(s32[64,2,1]{1,2,0:T(1,128)} %bitcast.4), calls=%async_computation.1 | async-start | bytes 65536 | tf_op jit(solution)/shard_map/all_to_all | solution.py:49
  31.2 12.7 %all-to-all-done.1 = s32[64,2,1]{1,2,0:T(1,128)S(1)} async-done(((s32[64,2,1]{1,2,0:T(1,128)}), s32[64,2,1]{1,2,0:T(1,128)S(1)}, u32[]{:S(2)}, u32[]{:S(2)}) %all-to-all-start.1) | async-done | bytes 544 | tf_op jit(solution)/shard_map/all_to_all | solution.py:49
  43.8 4.6 all-to-all-start
  48.4 2.1 gather_fusion.4
  50.6 11.4 %all-to-all-done = s32[64,2,1]{1,2,0:T(1,128)S(1)} async-done(((s32[64,2,1]{1,2,0:T(1,128)}), s32[64,2,1]{1,2,0:T(1,128)S(1)}, u32[]{:S(2)}, u32[]{:S(2)}) %all-to-all-start) | async-done | bytes 544 | tf_op jit(solution)/shard_map/all_to_all | solution.py:48
  61.9 4.7 all-to-all-start.3
  66.6 3.4 gather_fusion.2
  70.0 90.1 %all-to-all-done.3 = bf16[128,128,64]{1,2,0:T(8,128)(2,1)S(1)} async-done(((bf16[128,128,64]{1,2,0:T(8,128)(2,1)}), bf16[128,128,64]{1,2,0:T(8,128)(2,1)S(1)}, u32[]{:S(2)}, u32[]{:S(2)}) %all-to-all-start.3) | async-done | bytes 2097184 | tf_op jit(solution)/shard_map/all_to_all | solution.py:46
  160.2 1.3 copy-done.1
  161.5 10.7 %all-to-all-start.2 = ((bf16[128,128,64]{1,2,0:T(8,128)(2,1)}), bf16[128,128,64]{1,2,0:T(8,128)(2,1)S(1)}, u32[]{:S(2)}, u32[]{:S(2)}) async-start(bf16[128,128,64]{1,2,0:T(8,128)(2,1)} %gather_fusion.2), calls=%async_computation.2 | async-start | bytes 4194304 | tf_op jit(solution)/shard_map/all_to_all | solution.py:45
  172.9 1.3 gather_fusion.5
  176.7 34.6 %all-gather.2.cloned.1.call-done = bf16[160,64,64]{2,1,0:T(8,128)(2,1)} async-done(((bf16[20,64,64]{2,1,0:T(8,128)(2,1)}), bf16[160,64,64]{2,1,0:T(8,128)(2,1)}) %all-gather.2.cloned.1.call-update) | async-done | bytes 1310736 | tf_op jit(solution)/shard_map/all_gather | solution.py:39
  211.3 3.9 gather_fusion.3
  215.2 50.7 %all-to-all-done.2 = bf16[128,128,64]{1,2,0:T(8,128)(2,1)S(1)} async-done(((bf16[128,128,64]{1,2,0:T(8,128)(2,1)}), bf16[128,128,64]{1,2,0:T(8,128)(2,1)S(1)}, u32[]{:S(2)}, u32[]{:S(2)}) %all-to-all-start.2) | async-done | bytes 2097184 | tf_op jit(solution)/shard_map/all_to_all | solution.py:45
  265.9 11.0 %all-to-all-start.4 = ((bf16[64,2,128]{2,1,0:T(2,128)(2,1)}), bf16[64,2,128]{2,1,0:T(2,128)(2,1)S(1)}, u32[]{:S(2)}, u32[]{:S(2)}) async-start(bf16[64,2,128]{2,1,0:T(2,128)(2,1)} %bitcast.6), calls=%async_computation.4 | async-start | bytes 65536 | tf_op jit(solution)/shard_map/all_to_all | solution.py:47
  277.1 3.2 multiply_reduce_fusion
  280.4 9.9 %all-to-all-done.4 = bf16[64,2,128]{2,1,0:T(2,128)(2,1)S(1)} async-done(((bf16[64,2,128]{2,1,0:T(2,128)(2,1)}), bf16[64,2,128]{2,1,0:T(2,128)(2,1)S(1)}, u32[]{:S(2)}, u32[]{:S(2)}) %all-to-all-start.4) | async-done | bytes 32800 | tf_op jit(solution)/shard_map/all_to_all | solution.py:47
  290.4 4.8 fusion
  295.2 4.8 copy.30
  299.9 5.4 %fusion.1 = f32[160,64,64]{0,2,1:T(8,128)} fusion(f32[128,64,64]{0,2,1:T(8,128)} %copy.30, s32[128]{0:T(128)S(1)} %eq.50), kind=kOutput, calls=%fused_computation.12 | convolution fusion | flops 1006653440 | bytes 4719104 | tf_op jit(solution)/shard_map/dot_general | solution.py:53
  305.3 4.9 copy.26
  310.3 75.1 %all-reduce.2.cloned.1.call-done = f32[160,64,64]{0,2,1:T(8,128)} async-done(((f32[160,64,64]{0,2,1:T(8,128)}), f32[160,64,64]{0,2,1:T(8,128)}) %all-reduce.2.cloned.1.call-update) | async-done | bytes 2621456 | tf_op jit(solution)/shard_map/psum | solution.py:59
  385.4 5.0 subtract_convert_fusion
  390.4 5.0 copy.31
  395.4 3.9 gather_fusion.6
  399.3 3.8 convolution_convert_fusion
  403.0 15.8 %all-to-all-start.5 = ((bf16[128,128,64]{1,2,0:T(8,128)(2,1)}), bf16[128,128,64]{1,2,0:T(8,128)(2,1)}, u32[]{:S(2)}, u32[]{:S(2)}) async-start(bf16[128,128,64]{1,2,0:T(8,128)(2,1)} %convolution_convert_fusion), calls=%async_computation.5 | async-start | bytes 4194304 | tf_op jit(solution)/shard_map/all_to_all | solution.py:67
  418.8 1.5 constant_dynamic-slice_fusion
  420.3 2.6 copy.33
  422.8 95.4 %all-to-all-done.5 = bf16[128,128,64]{1,2,0:T(8,128)(2,1)} async-done(((bf16[128,128,64]{1,2,0:T(8,128)(2,1)}), bf16[128,128,64]{1,2,0:T(8,128)(2,1)}, u32[]{:S(2)}, u32[]{:S(2)}) %all-to-all-start.5) | async-done | bytes 2097184 | tf_op jit(solution)/shard_map/all_to_all | solution.py:67
  518.3 3.2 gather_fusion.7
  (33 shorter events, 7.4 us)
Async XLA Ops:
  7.2 41.3 %copy-start = (bf16[64,128,64]{1,2,0:T(8,128)(2,1)S(1)}, bf16[64,128,64]{1,2,0:T(8,128)(2,1)}, u32[]{:S(2)}) copy-start(bf16[64,128,64]{1,2,0:T(8,128)(2,1)} %param.7) | copy-start | bytes 3145732
  12.0 31.9 %all-to-all-start.1 = ((s32[64,2,1]{1,2,0:T(1,128)}), s32[64,2,1]{1,2,0:T(1,128)S(1)}, u32[]{:S(2)}, u32[]{:S(2)}) async-start(s32[64,2,1]{1,2,0:T(1,128)} %bitcast.4), calls=%async_computation.1 | async-start | bytes 65536 | tf_op jit(solution)/shard_map/all_to_all | solution.py:49
  43.8 18.1 %all-to-all-start = ((s32[64,2,1]{1,2,0:T(1,128)}), s32[64,2,1]{1,2,0:T(1,128)S(1)}, u32[]{:S(2)}, u32[]{:S(2)}) async-start(s32[64,2,1]{1,2,0:T(1,128)} %bitcast.2), calls=%async_computation | async-start | bytes 65536 | tf_op jit(solution)/shard_map/all_to_all | solution.py:48
  61.9 98.2 %all-to-all-start.3 = ((bf16[128,128,64]{1,2,0:T(8,128)(2,1)}), bf16[128,128,64]{1,2,0:T(8,128)(2,1)S(1)}, u32[]{:S(2)}, u32[]{:S(2)}) async-start(bf16[128,128,64]{1,2,0:T(8,128)(2,1)} %gather_fusion.4), calls=%async_computation.3 | async-start | bytes 4194304 | tf_op jit(solution)/shard_map/all_to_all | solution.py:46
  70.0 102.9 %copy-start.3 = (bf16[64,128]{1,0:T(8,128)(2,1)S(1)}, bf16[64,128]{1,0:T(8,128)(2,1)}, u32[]{:S(2)}) copy-start(bf16[64,128]{1,0:T(8,128)(2,1)} %param.8) | copy-start | bytes 49156
  160.2 1.3 copy-start.1
  161.5 104.4 %all-to-all-start.2 = ((bf16[128,128,64]{1,2,0:T(8,128)(2,1)}), bf16[128,128,64]{1,2,0:T(8,128)(2,1)S(1)}, u32[]{:S(2)}, u32[]{:S(2)}) async-start(bf16[128,128,64]{1,2,0:T(8,128)(2,1)} %gather_fusion.2), calls=%async_computation.2 | async-start | bytes 4194304 | tf_op jit(solution)/shard_map/all_to_all | solution.py:45
  172.2 39.1 %all-gather.2.cloned.1.call-start = ((), (), s32[]{:S(2)}) async-start(), calls=%async_computation.6 | async-start | bytes 2949120 | tf_op jit(solution)/shard_map/all_gather | solution.py:39
  265.9 24.4 %all-to-all-start.4 = ((bf16[64,2,128]{2,1,0:T(2,128)(2,1)}), bf16[64,2,128]{2,1,0:T(2,128)(2,1)S(1)}, u32[]{:S(2)}, u32[]{:S(2)}) async-start(bf16[64,2,128]{2,1,0:T(2,128)(2,1)} %bitcast.6), calls=%async_computation.4 | async-start | bytes 65536 | tf_op jit(solution)/shard_map/all_to_all | solution.py:47
  276.9 108.5 %all-reduce.2.cloned.1.call-start = ((), (), s32[]{:S(2)}) async-start(), calls=%async_computation.7 | async-start | bytes 8388608 | tf_op jit(solution)/shard_map/psum | solution.py:59
  403.0 15.8 %copy-start.2 = (bf16[160,64,64]{0,2,1:T(8,128)(2,1)S(1)}, bf16[160,64,64]{0,2,1:T(8,128)(2,1)}, u32[]{:S(2)}) copy-start(bf16[160,64,64]{0,2,1:T(8,128)(2,1)} %subtract_convert_fusion) | copy-start | bytes 3932164
  403.0 115.2 %all-to-all-start.5 = ((bf16[128,128,64]{1,2,0:T(8,128)(2,1)}), bf16[128,128,64]{1,2,0:T(8,128)(2,1)}, u32[]{:S(2)}, u32[]{:S(2)}) async-start(bf16[128,128,64]{1,2,0:T(8,128)(2,1)} %convolution_convert_fusion), calls=%async_computation.5 | async-start | bytes 4194304 | tf_op jit(solution)/shard_map/all_to_all | solution.py:67
Sparse Core Ops, SparseCore 0:
  175.1 36.1 all-gather.1
  305.5 79.8 all-reduce.1
where the time goes:
time: 529 us; the launch traced here: 528 us
  waiting for transfers between devices  381 us (72%)
  starting transfers between devices  65.5 us (12%)
  local copies, waits for them, and re-layouts  43.1 us (8%)
  matrix products  17.1 us (3%)
  between operations  14.2 us (3%)
  other arithmetic  7.74 us (1%)
    all_to_all x1, waiting for transfers between devices, body(): lax.all_to_all(refreshed, 'own', split_axis=0, concat_axis=0, tiled=True)  95.4 us
    all_to_all x1, waiting for transfers between devices, body(): lax.all_to_all(send_right, 'own', split_axis=0, concat_axis=0, tiled=True)  90.1 us
    psum x1, waiting for transfers between devices, body(): grad_whole = lax.psum(grad_part, 'grp')  75.1 us
    all_to_all x1, waiting for transfers between devices, body(): lax.all_to_all(send_left, 'own', split_axis=0, concat_axis=0, tiled=True)  50.7 us
    all_gather x1, waiting for transfers between devices, body(): old_tables = lax.all_gather(core, 'grp', axis=0, tiled=True)  34.6 us
    all_to_all x1, starting transfers between devices, body(): lax.all_to_all(send_fill, 'own', split_axis=0, concat_axis=0, tiled=True)  18.5 us
    all_to_all x1, starting transfers between devices, body(): lax.all_to_all(refreshed, 'own', split_axis=0, concat_axis=0, tiled=True)  15.8 us
    all_to_all x1, waiting for transfers between devices, body(): lax.all_to_all(send_fill, 'own', split_axis=0, concat_axis=0, tiled=True)  12.7 us
  transfers between devices with their start and end apart: 8, of which 8 were waited for; matrix products, arithmetic and copies ran while one was open for 5% of the time, Pallas kernels for 0%

commit v1 on v0

--- a/solution.py
+++ b/solution.py
@@ -36,7 +36,9 @@
     slot_live = jnp.any(slot_match, axis=1)
     tile_of_slot = jnp.sum(jnp.where(slot_match, positions[None, :], 0), axis=1)
     send_slice = jnp.where(slot_live, local_slice[tile_of_slot], 0)
-    old_tables = lax.all_gather(core, "grp", axis=0, tiled=True)
+    old_tables = jnp.concatenate(
+        lax.all_to_all(jnp.stack([core] * lax.axis_size("grp")), "grp", 0, 0), axis=0
+    )
     send_left = left[tile_of_slot]
     send_right = right[tile_of_slot]
     send_values = values[tile_of_slot]

time: 529 us -> 559 us (1.057)
  local copies, waits for them, and re-layouts: 43.1 us -> 56.6 us
  starting transfers between devices: 65.5 us -> 75.6 us
    all_gather x1 -> x0, waiting for transfers between devices: 34.6 us -> none  [body(): old_tables = lax.all_gather(core, 'grp', axis=0, tiled=True)]
    all_to_all x1, waiting for transfers between devices: 50.7 us -> 82.6 us  [body(): lax.all_to_all(send_left, 'own', split_axis=0, concat_axis=0, tiled=True)]
    all_to_all x0 -> x1, waiting for transfers between devices: none -> 14 us  [body(): lax.all_to_all(jnp.stack([core] * lax.axis_size('grp')), 'grp', 0, 0)]
    unnamed x9 -> x13, local copies, waits for them, and re-layouts: 3.89 us -> 14.2 us
    all_to_all x0 -> x1, starting transfers between devices: none -> 7.71 us  [body(): lax.all_to_all(jnp.stack([core] * lax.axis_size('grp')), 'grp', 0, 0)]
    all_to_all x1, waiting for transfers between devices: 11.4 us -> 5.75 us  [body(): lax.all_to_all(send_slice, 'own', split_axis=0, concat_axis=0, tiled=True)]
  transfers between devices with their start and end apart: 8 -> 8, of which waited for: 8 -> 8; matrix products, arithmetic and copies ran while one was open for 5% -> 7% of each run, Pallas kernels for 0% -> 0%
where the time goes in v1:
time: 559 us; the launch traced here: 557 us
  waiting for transfers between devices  386 us (69%)
  starting transfers between devices  75.6 us (14%)
  local copies, waits for them, and re-layouts  56.6 us (10%)
  matrix products  17.1 us (3%)
  between operations  14.2 us (3%)
  other arithmetic  7.74 us (1%)
    all_to_all x1, waiting for transfers between devices, body(): lax.all_to_all(refreshed, 'own', split_axis=0, concat_axis=0, tiled=True)  95.4 us
    all_to_all x1, waiting for transfers between devices, body(): lax.all_to_all(send_right, 'own', split_axis=0, concat_axis=0, tiled=True)  91.3 us
    all_to_all x1, waiting for transfers between devices, body(): lax.all_to_all(send_left, 'own', split_axis=0, concat_axis=0, tiled=True)  82.6 us
    psum x1, waiting for transfers between devices, body(): grad_whole = lax.psum(grad_part, 'grp')  74.5 us
    all_to_all x1, starting transfers between devices, body(): lax.all_to_all(send_fill, 'own', split_axis=0, concat_axis=0, tiled=True)  18.5 us
    all_to_all x1, starting transfers between devices, body(): lax.all_to_all(refreshed, 'own', split_axis=0, concat_axis=0, tiled=True)  15.8 us
    unnamed x13, local copies, waits for them, and re-layouts  14.2 us
    all_to_all x1, waiting for transfers between devices, body(): lax.all_to_all(jnp.stack([core] * lax.axis_size('grp')), 'grp', 0, 0)  14 us
  transfers between devices with their start and end apart: 8, of which 8 were waited for; matrix products, arithmetic and copies ran while one was open for 7% of the time, Pallas kernels for 0%

profile of v1, /device:TPU:7, one launch (start us, length us, event | category | flops | bytes accessed | tf_op | source)
XLA Modules:
  0.0 557.4 jit_solution(3237063864005066337)
XLA Ops:
  12.0 18.5 %all-to-all-start.2 = ((s32[64,2,1]{1,2,0:T(1,128)}), s32[64,2,1]{1,2,0:T(1,128)S(1)}, u32[]{:S(2)}, u32[]{:S(2)}) async-start(s32[64,2,1]{1,2,0:T(1,128)} %bitcast.5), calls=%async_computation.2 | async-start | bytes 65536 | tf_op jit(solution)/shard_map/all_to_all | solution.py:51
  31.2 12.7 %all-to-all-done.2 = s32[64,2,1]{1,2,0:T(1,128)S(1)} async-done(((s32[64,2,1]{1,2,0:T(1,128)}), s32[64,2,1]{1,2,0:T(1,128)S(1)}, u32[]{:S(2)}, u32[]{:S(2)}) %all-to-all-start.2) | async-done | bytes 544 | tf_op jit(solution)/shard_map/all_to_all | solution.py:51
  43.8 4.6 all-to-all-start.1
  48.4 3.1 stack.2
  51.6 4.6 reshape.228
  56.2 5.8 %all-to-all-done.1 = s32[64,2,1]{1,2,0:T(1,128)S(1)} async-done(((s32[64,2,1]{1,2,0:T(1,128)}), s32[64,2,1]{1,2,0:T(1,128)S(1)}, u32[]{:S(2)}, u32[]{:S(2)}) %all-to-all-start.1) | async-done | bytes 544 | tf_op jit(solution)/shard_map/all_to_all | solution.py:50
  61.9 7.7 %all-to-all-start = ((bf16[8,2,40960]{2,1,0:T(2,128)(2,1)}), bf16[8,2,40960]{2,1,0:T(2,128)(2,1)S(1)}, u32[]{:S(2)}, u32[]{:S(2)}) async-start(bf16[8,2,40960]{2,1,0:T(2,128)(2,1)} %reshape.228), calls=%async_computation | async-start | bytes 2621440 | tf_op jit(solution)/shard_map/all_to_all | solution.py:40
  69.7 2.1 gather_fusion.4
  71.8 14.0 %all-to-all-done = bf16[8,2,40960]{2,1,0:T(2,128)(2,1)S(1)} async-done(((bf16[8,2,40960]{2,1,0:T(2,128)(2,1)}), bf16[8,2,40960]{2,1,0:T(2,128)(2,1)S(1)}, u32[]{:S(2)}, u32[]{:S(2)}) %all-to-all-start) | async-done | bytes 1310752 | tf_op jit(solution)/shard_map/all_to_all | solution.py:40
  86.8 7.8 %all-to-all-start.4 = ((bf16[128,128,64]{1,2,0:T(8,128)(2,1)}), bf16[128,128,64]{1,2,0:T(8,128)(2,1)S(1)}, u32[]{:S(2)}, u32[]{:S(2)}) async-start(bf16[128,128,64]{1,2,0:T(8,128)(2,1)} %gather_fusion.4), calls=%async_computation.4 | async-start | bytes 4194304 | tf_op jit(solution)/shard_map/all_to_all | solution.py:48
  94.7 3.4 gather_fusion.2
  98.0 91.3 %all-to-all-done.4 = bf16[128,128,64]{1,2,0:T(8,128)(2,1)S(1)} async-done(((bf16[128,128,64]{1,2,0:T(8,128)(2,1)}), bf16[128,128,64]{1,2,0:T(8,128)(2,1)S(1)}, u32[]{:S(2)}, u32[]{:S(2)}) %all-to-all-start.4) | async-done | bytes 2097184 | tf_op jit(solution)/shard_map/all_to_all | solution.py:48
  190.7 10.8 %all-to-all-start.3 = ((bf16[128,128,64]{1,2,0:T(8,128)(2,1)}), bf16[128,128,64]{1,2,0:T(8,128)(2,1)S(1)}, u32[]{:S(2)}, u32[]{:S(2)}) async-start(bf16[128,128,64]{1,2,0:T(8,128)(2,1)} %gather_fusion.2), calls=%async_computation.3 | async-start | bytes 4194304 | tf_op jit(solution)/shard_map/all_to_all | solution.py:47
  205.2 4.7 reshape.229
  209.9 3.9 gather_fusion.3
  213.8 82.6 %all-to-all-done.3 = bf16[128,128,64]{1,2,0:T(8,128)(2,1)S(1)} async-done(((bf16[128,128,64]{1,2,0:T(8,128)(2,1)}), bf16[128,128,64]{1,2,0:T(8,128)(2,1)S(1)}, u32[]{:S(2)}, u32[]{:S(2)}) %all-to-all-start.3) | async-done | bytes 2097184 | tf_op jit(solution)/shard_map/all_to_all | solution.py:47
  296.4 10.2 %all-to-all-start.5 = ((bf16[64,2,128]{2,1,0:T(2,128)(2,1)}), bf16[64,2,128]{2,1,0:T(2,128)(2,1)S(1)}, u32[]{:S(2)}, u32[]{:S(2)}) async-start(bf16[64,2,128]{2,1,0:T(2,128)(2,1)} %bitcast.7), calls=%async_computation.5 | async-start | bytes 65536 | tf_op jit(solution)/shard_map/all_to_all | solution.py:49
  306.8 3.2 multiply_reduce_fusion
  310.1 9.9 %all-to-all-done.5 = bf16[64,2,128]{2,1,0:T(2,128)(2,1)S(1)} async-done(((bf16[64,2,128]{2,1,0:T(2,128)(2,1)}), bf16[64,2,128]{2,1,0:T(2,128)(2,1)S(1)}, u32[]{:S(2)}, u32[]{:S(2)}) %all-to-all-start.5) | async-done | bytes 32800 | tf_op jit(solution)/shard_map/all_to_all | solution.py:49
  320.1 4.8 fusion
  324.8 4.8 copy.29
  329.6 5.4 fusion.1
  335.0 4.9 copy.25
  339.9 74.5 %all-reduce.2.cloned.1.call-done = f32[160,64,64]{0,2,1:T(8,128)} async-done(((f32[160,64,64]{0,2,1:T(8,128)}), f32[160,64,64]{0,2,1:T(8,128)}) %all-reduce.2.cloned.1.call-update) | async-done | bytes 2621456 | tf_op jit(solution)/shard_map/psum | solution.py:61
  414.4 5.0 subtract_convert_fusion
  419.4 5.0 copy.30
  424.4 3.9 gather_fusion.6
  428.3 3.8 convolution_convert_fusion
  432.1 15.8 %all-to-all-start.6 = ((bf16[128,128,64]{1,2,0:T(8,128)(2,1)}), bf16[128,128,64]{1,2,0:T(8,128)(2,1)}, u32[]{:S(2)}, u32[]{:S(2)}) async-start(bf16[128,128,64]{1,2,0:T(8,128)(2,1)} %convolution_convert_fusion), calls=%async_computation.6 | async-start | bytes 4194304 | tf_op jit(solution)/shard_map/all_to_all | solution.py:69
  449.3 2.6 copy.32
  451.9 95.4 %all-to-all-done.6 = bf16[128,128,64]{1,2,0:T(8,128)(2,1)} async-done(((bf16[128,128,64]{1,2,0:T(8,128)(2,1)}), bf16[128,128,64]{1,2,0:T(8,128)(2,1)}, u32[]{:S(2)}, u32[]{:S(2)}) %all-to-all-start.6) | async-done | bytes 2097184 | tf_op jit(solution)/shard_map/all_to_all | solution.py:69
  547.3 3.2 gather_fusion.7
  (37 shorter events, 13.4 us)
Async XLA Ops:
  7.2 62.5 %copy-start = (bf16[64,128,64]{1,2,0:T(8,128)(2,1)S(1)}, bf16[64,128,64]{1,2,0:T(8,128)(2,1)}, u32[]{:S(2)}) copy-start(bf16[64,128,64]{1,2,0:T(8,128)(2,1)} %param.7) | copy-start | bytes 3145732
  12.0 31.9 %all-to-all-start.2 = ((s32[64,2,1]{1,2,0:T(1,128)}), s32[64,2,1]{1,2,0:T(1,128)S(1)}, u32[]{:S(2)}, u32[]{:S(2)}) async-start(s32[64,2,1]{1,2,0:T(1,128)} %bitcast.5), calls=%async_computation.2 | async-start | bytes 65536 | tf_op jit(solution)/shard_map/all_to_all | solution.py:51
  43.8 18.1 %all-to-all-start.1 = ((s32[64,2,1]{1,2,0:T(1,128)}), s32[64,2,1]{1,2,0:T(1,128)S(1)}, u32[]{:S(2)}, u32[]{:S(2)}) async-start(s32[64,2,1]{1,2,0:T(1,128)} %bitcast.3), calls=%async_computation.1 | async-start | bytes 65536 | tf_op jit(solution)/shard_map/all_to_all | solution.py:50
  61.9 23.8 %all-to-all-start = ((bf16[8,2,40960]{2,1,0:T(2,128)(2,1)}), bf16[8,2,40960]{2,1,0:T(2,128)(2,1)S(1)}, u32[]{:S(2)}, u32[]{:S(2)}) async-start(bf16[8,2,40960]{2,1,0:T(2,128)(2,1)} %reshape.228), calls=%async_computation | async-start | bytes 2621440 | tf_op jit(solution)/shard_map/all_to_all | solution.py:40
  85.8 1.1 copy-start.3
  86.8 102.6 %all-to-all-start.4 = ((bf16[128,128,64]{1,2,0:T(8,128)(2,1)}), bf16[128,128,64]{1,2,0:T(8,128)(2,1)S(1)}, u32[]{:S(2)}, u32[]{:S(2)}) async-start(bf16[128,128,64]{1,2,0:T(8,128)(2,1)} %gather_fusion.4), calls=%async_computation.4 | async-start | bytes 4194304 | tf_op jit(solution)/shard_map/all_to_all | solution.py:48
  98.0 103.4 %copy-start.4 = (bf16[64,128]{1,0:T(8,128)(2,1)S(1)}, bf16[64,128]{1,0:T(8,128)(2,1)}, u32[]{:S(2)}) copy-start(bf16[64,128]{1,0:T(8,128)(2,1)} %param.8) | copy-start | bytes 49156
  189.4 1.3 copy-start.1
  190.7 105.7 %all-to-all-start.3 = ((bf16[128,128,64]{1,2,0:T(8,128)(2,1)}), bf16[128,128,64]{1,2,0:T(8,128)(2,1)S(1)}, u32[]{:S(2)}, u32[]{:S(2)}) async-start(bf16[128,128,64]{1,2,0:T(8,128)(2,1)} %gather_fusion.2), calls=%async_computation.3 | async-start | bytes 4194304 | tf_op jit(solution)/shard_map/all_to_all | solution.py:47
  296.4 23.6 %all-to-all-start.5 = ((bf16[64,2,128]{2,1,0:T(2,128)(2,1)}), bf16[64,2,128]{2,1,0:T(2,128)(2,1)S(1)}, u32[]{:S(2)}, u32[]{:S(2)}) async-start(bf16[64,2,128]{2,1,0:T(2,128)(2,1)} %bitcast.7), calls=%async_computation.5 | async-start | bytes 65536 | tf_op jit(solution)/shard_map/all_to_all | solution.py:49
  306.6 107.8 %all-reduce.2.cloned.1.call-start = ((), (), s32[]{:S(2)}) async-start(), calls=%async_computation.7 | async-start | bytes 8388608 | tf_op jit(solution)/shard_map/psum | solution.py:61
  432.1 15.8 %copy-start.2 = (bf16[160,64,64]{0,2,1:T(8,128)(2,1)S(1)}, bf16[160,64,64]{0,2,1:T(8,128)(2,1)}, u32[]{:S(2)}) copy-start(bf16[160,64,64]{0,2,1:T(8,128)(2,1)} %subtract_convert_fusion) | copy-start | bytes 3932164
  432.1 115.2 %all-to-all-start.6 = ((bf16[128,128,64]{1,2,0:T(8,128)(2,1)}), bf16[128,128,64]{1,2,0:T(8,128)(2,1)}, u32[]{:S(2)}, u32[]{:S(2)}) async-start(bf16[128,128,64]{1,2,0:T(8,128)(2,1)} %convolution_convert_fusion), calls=%async_computation.6 | async-start | bytes 4194304 | tf_op jit(solution)/shard_map/all_to_all | solution.py:69
Sparse Core Ops, SparseCore 0:
  335.2 79.2 all-reduce.1
